TPU v7x, 128 devices: a whole 4x4x4 slice. The times are simulated.
128 devices in a mesh: aa: 16 (over y, x), ba: 8 (over z, core).
Axes of the slice: x: 4, y: 4, z: 4, core: 2. Of those that a mesh axis runs over, the one named last changes fastest.
Arguments:
- queries: bfloat16 [8, 128, 8192], P('ba', None, 'aa'), may hold values from -10 to 10
- new_kv: bfloat16 [8, 128, 2, 512], P('ba', 'aa'), may hold values from -4 to 4
- pool: bfloat16 [8, 192, 32, 2, 512], P('ba', 'aa'), may hold values from -4 to 4
- page_table: int32 [8, 64], P('ba', 'aa'), may hold values from 0 to 11, as said below
- ctx_len: int32 [8, 16], P('ba', 'aa'), may hold values from 1 to 128, as said below
- move_page: int32 [8, 112], P('ba', 'aa'), may hold values from 0 to 11, as said below
- move_dest: int32 [8, 112], P('ba', 'aa'), may hold values from 0 to 7, as said below
- append_page: int32 [8, 16], P('ba', 'aa'), may hold values from 0 to 11
Outputs:
- attended: bfloat16 [8, 128, 8192], P('ba', None, 'aa')
- pool_out: bfloat16 [8, 192, 32, 2, 512], P('ba', 'aa')
Inputs may be any that keep to these rules, and one draw needn't show every extreme that they name: `page_table`: the entries of one device are distinct pages of its pool and differ from its leaving pages and its append page. `ctx_len`: for each instance some index of aa holds exactly 128 live rows. `move_page`: the 7 entries of one device are distinct pages of its pool. `move_dest`: A device never names its own instance and names any one instance at most 2 times; for each index of aa one instance is named exactly 2 times by the device of every other instance.
All inputs are finite; a program needn't handle non-finite values.
Results may differ from a plain program's by a relative error of at most 0.0017.
Values may be sent and summed in bfloat16 or wider, within the bound.
No kernel may reach another device: no remote copies, remote signals or barrier semaphores. Data moves between devices by JAX's collectives and lax.ppermute only.
A program may use at most 64 MiB of HBM per device.

v0:
```python
import math
import jax
import jax.numpy as jnp
from jax import lax
from jax.sharding import PartitionSpec as P

HEAD_DIM = 128
MOST = 2
NEG_LARGE = -1e30


def in_one_piece(arrays, axis, split_dim, concat_dim, along):
    widths = [math.prod(a.shape[along:]) for a in arrays]
    both = jnp.concatenate(
        [a.reshape(*a.shape[:along], w) for a, w in zip(arrays, widths)], axis=along
    )
    filled = lax.all_to_all(both, axis, split_axis=split_dim, concat_axis=concat_dim, tiled=True)
    blocks = jnp.split(filled, [sum(widths[:k]) for k in range(1, len(widths))], axis=along)
    return tuple(
        (b.reshape(*filled.shape[:along], *a.shape[along:]) for a, b in zip(arrays, blocks))
    )


def from_everyone(value, axis):
    length = lax.axis_size(axis)
    return lax.all_to_all(
        jnp.broadcast_to(value[None], (length, *value.shape)), axis, 0, 0, tiled=True
    )


def taken_together(value, axis):
    return from_everyone(value, axis).max(axis=0)


def split_up(value, dim, length):
    lengths = value.shape
    blocks = value.reshape(*lengths[:dim], length, lengths[dim] // length, *lengths[dim + 1 :])
    return jnp.moveaxis(blocks, dim, 0)


def sum_at_owner(value, axis, dim):
    length = lax.axis_size(axis)
    blocks = lax.all_to_all(split_up(value, dim, length), axis, 0, 0, tiled=True)
    return jnp.sum(blocks, axis=0)


def in_one_piece_2(arrays, axis, dim, along):
    widths = [math.prod(a.shape[along:]) for a in arrays]
    both = jnp.concatenate(
        [a.reshape(*a.shape[:along], w) for a, w in zip(arrays, widths)], axis=along
    )
    filled = sum_at_owner(both, axis, dim)
    blocks = jnp.split(filled, [sum(widths[:k]) for k in range(1, len(widths))], axis=along)
    return tuple(
        (b.reshape(*filled.shape[:along], *a.shape[along:]) for a, b in zip(arrays, blocks))
    )


def block_plan(total_rows):
    counted = max(1, total_rows // 512)
    length = -(-total_rows // counted)
    length = -(-length // 8) * 8
    return (counted, length)


def combine_parts(former, latter):
    former_max, former_sum, former_out = former
    latter_max, latter_sum, latter_out = latter
    joint_max = jnp.maximum(former_max, latter_max)
    former_scale = jnp.exp(former_max - joint_max)
    latter_scale = jnp.exp(latter_max - joint_max)
    joint_sum = former_sum * former_scale + latter_sum * latter_scale
    joint_out = former_out * former_scale[..., None] + latter_out * latter_scale[..., None]
    return (joint_max, joint_sum, joint_out)


def attend_rows(query_heads, key_rows, visible):
    total_rows = key_rows.shape[0]
    counted, length = block_plan(total_rows)
    query_count, kv_heads, group_size, head_dim = query_heads.shape
    blocked_keys = key_rows.reshape(counted, length, 2, kv_heads, head_dim)
    blocked_mask = visible.reshape(query_count, counted, length).transpose(1, 0, 2)
    scale = 1.0 / math.sqrt(head_dim)

    def block_step(state_now, inputs):
        run_max, run_sum, run_out = state_now
        block_keys, block_mask = inputs
        scores = (
            jnp.einsum(
                "qkgd,rkd->qkgr", query_heads, block_keys[:, 0], preferred_element_type=jnp.float32
            )
            * scale
        )
        allowed = block_mask[:, None, None, :]
        scores = jnp.where(allowed, scores, NEG_LARGE)
        new_max = jnp.maximum(run_max, jnp.max(scores, axis=-1))
        weights = jnp.where(allowed, jnp.exp(scores - new_max[..., None]), 0.0)
        shrink = jnp.exp(run_max - new_max)
        new_sum = run_sum * shrink + jnp.sum(weights, axis=-1)
        block_values = block_keys[:, 1].astype(jnp.float32)
        new_out = run_out * shrink[..., None] + jnp.einsum(
            "qkgr,rkd->qkgd", weights, block_values, precision=lax.Precision.HIGHEST
        )
        return ((new_max, new_sum, new_out), None)

    start_state = (
        jnp.full((query_count, kv_heads, group_size), NEG_LARGE, jnp.float32),
        jnp.zeros((query_count, kv_heads, group_size), jnp.float32),
        jnp.zeros((query_count, kv_heads, group_size, head_dim), jnp.float32),
    )
    finished, _ = lax.scan(block_step, start_state, (blocked_keys, blocked_mask))
    return finished


def local(queries, new_kv, pool, page_table, ctx_len, move_page, move_dest, append_page):
    instances = lax.axis_size("ba")
    position = lax.axis_index("aa")
    pool_pages = pool[0]
    page_rows = pool_pages.shape[1]
    kv_width = pool_pages.shape[-1]
    kv_heads = kv_width // HEAD_DIM
    gathered = lax.all_gather(queries[0], "aa", axis=1, tiled=True)
    query_count = gathered.shape[0]
    query_heads = gathered.reshape(query_count, kv_heads, -1, HEAD_DIM)
    moved_ids = move_page[0]
    targets = move_dest[0]
    move_count = moved_ids.shape[0]
    counter = jnp.arange(move_count, dtype=jnp.int32)
    earlier = (counter[None, :] < counter[:, None]) & (targets[None, :] == targets[:, None])
    slot_index = targets * MOST + jnp.sum(earlier, axis=1)
    select = (jnp.arange(instances * MOST, dtype=jnp.int32)[:, None] == slot_index[None, :]).astype(
        jnp.bfloat16
    )
    picked = jnp.take(pool_pages, moved_ids, axis=0).reshape(move_count, -1)
    outgoing = jnp.dot(select, picked, preferred_element_type=jnp.float32).astype(jnp.bfloat16)
    outgoing = outgoing.reshape(instances, MOST, page_rows, 2, kv_width)
    occupied = (
        jnp.sum(select.astype(jnp.float32), axis=1).astype(jnp.bfloat16).reshape(instances, MOST)
    )
    incoming, arrived = in_one_piece((outgoing, occupied), "ba", 0, 0, 2)
    moved_rows = incoming.reshape(-1, 2, kv_width)
    moved_live = jnp.broadcast_to(
        (arrived > 0.5)[:, :, None], (instances, MOST, page_rows)
    ).reshape(-1)
    resident = jnp.take(pool_pages, page_table[0], axis=0).reshape(-1, 2, kv_width)
    resident_live = jnp.arange(resident.shape[0], dtype=jnp.int32) < ctx_len[0, 0]
    fresh_rows = new_kv[0]
    fresh_count = fresh_rows.shape[0]
    fresh_place = position * fresh_count + jnp.arange(fresh_count, dtype=jnp.int32)
    fresh_visible = fresh_place[None, :] <= jnp.arange(query_count, dtype=jnp.int32)[:, None]
    resident_visible = jnp.broadcast_to(
        resident_live[None, :], (query_count, resident_live.shape[0])
    )
    moved_visible = jnp.broadcast_to(moved_live[None, :], (query_count, moved_live.shape[0]))
    local_part = attend_rows(
        query_heads,
        jnp.concatenate([resident, fresh_rows], axis=0),
        jnp.concatenate([resident_visible, fresh_visible], axis=1),
    )
    moved_part = attend_rows(query_heads, moved_rows, moved_visible)
    partials = combine_parts(local_part, moved_part)
    run_max, run_sum, run_out = partials
    top_max = taken_together(run_max, "aa")
    rescale = jnp.exp(run_max - top_max)
    numerator = (run_out * rescale[..., None]).reshape(query_count, -1, HEAD_DIM)
    denominator = (run_sum * rescale).reshape(query_count, -1)
    numerator, denominator = in_one_piece_2((numerator, denominator), "aa", 1, 2)
    result = numerator / denominator[..., None]
    attended = result.reshape(1, query_count, -1).astype(jnp.bfloat16)
    zero = jnp.zeros((), jnp.int32)
    updated = lax.dynamic_update_slice(
        pool_pages, fresh_rows[None], (append_page[0, 0], zero, zero, zero)
    )
    return (attended, updated[None])


def solution(mesh):
    return jax.shard_map(
        local,
        mesh=mesh,
        in_specs=(
            P("ba", None, "aa"),
            P("ba", "aa", None, None),
            P("ba", "aa", None, None, None),
            P("ba", "aa"),
            P("ba", "aa"),
            P("ba", "aa"),
            P("ba", "aa"),
            P("ba", "aa"),
        ),
        out_specs=(P("ba", None, "aa"), P("ba", "aa", None, None, None)),
        check_vma=False,
    )
```

profile of v0, /device:TPU:0, one launch (start us, length us, event | category | flops | bytes accessed | tf_op | source)
XLA Modules:
  0.0 190.3 jit_solution(174172654630481055)
XLA Ops:
  7.2 0.0 all-gather.3.cloned.1.call-start
  7.2 1.1 copy.173
  8.3 1.7 copy.132
  10.0 0.0 all-gather.3.cloned.1.call-update
  10.0 0.7 fusion.45
  10.7 0.7 compare_and_fusion
  11.4 0.9 convert_reduce_fusion
  12.3 0.7 fusion.46
  12.9 0.1 fusion.42
  13.0 0.1 reshape_reshape.9
  13.1 1.5 gather_fusion.1
  14.6 0.0 copy-start.4
  14.6 0.0 copy-start.3
  14.6 0.3 gather.15
  14.9 0.6 convolution_convert_fusion
  15.5 0.7 reshape_reshape.7
  16.2 1.9 %pad_maximum_fusion = bf16[8,2,32769]{2,1,0:T(2,128)(2,1)} fusion(bf16[8,2,1]{2,1,0:T(2,128)(2,1)S(1)} %reshape_reshape.9, bf16[8,2,32768]{2,1,0:T(2,128)(2,1)S(1)} %reshape_reshape.7), kind=kLoop, calls=%fused_computation.33 | loop fusion | flops 2097216 | bytes 2097216 | tf_op jit(solution)/shard_map/concatenate | solution.py:14
  18.2 5.4 %all-to-all-start = ((bf16[8,2,32769]{2,1,0:T(2,128)(2,1)}), bf16[8,2,32769]{2,1,0:T(2,128)(2,1)S(1)}, u32[]{:S(2)}, u32[]{:S(2)}) async-start(bf16[8,2,32769]{2,1,0:T(2,128)(2,1)} %pad_maximum_fusion), calls=%async_computation | async-start | bytes 2105344 | tf_op jit(solution)/shard_map/all_to_all | solution.py:17
  23.6 0.0 copy-done.4
  24.3 0.1 broadcast_in_dim.123
  24.4 0.1 broadcast_in_dim.124
  24.4 0.0 copy-done.3
  24.5 1.1 gather_fusion
  25.6 0.2 reshape.297
  25.8 0.1 iota_compare_fusion.3
  25.8 0.1 pad_add_fusion
  25.9 0.1 copy_select_fusion
  26.0 13.6 %all-to-all-done = bf16[8,2,32769]{2,1,0:T(2,128)(2,1)S(1)} async-done(((bf16[8,2,32769]{2,1,0:T(2,128)(2,1)}), bf16[8,2,32769]{2,1,0:T(2,128)(2,1)S(1)}, u32[]{:S(2)}, u32[]{:S(2)}) %all-to-all-start) | async-done | bytes 1048640 | tf_op jit(solution)/shard_map/all_to_all | solution.py:17
  39.6 0.1 copy.156
  39.7 0.7 split.17
  40.4 0.8 squeeze.63
  41.3 0.4 fusion.58
  41.6 1.1 copy.158
  42.8 0.1 copy.136
  42.9 0.1 broadcast_in_dim.132
  42.9 0.1 broadcast_in_dim.133
  43.0 15.0 %all-gather.3.cloned.1.call-done = bf16[1,128,8192]{1,2,0:T(8,128)(2,1)} async-done(((bf16[1,128,512]{1,2,0:T(8,128)(2,1)}), bf16[1,128,8192]{1,2,0:T(8,128)(2,1)}) %all-gather.3.cloned.1.call-update) | async-done | bytes 2097168 | tf_op jit(solution)/shard_map/all_gather | solution.py:122
  58.0 0.0 copy-start
  58.1 8.9 %bitcast_reduce_fusion = (f32[128,4,16]{0,2,1:T(8,128)S(1)}, f32[4,512,128,16]{2,1,3,0:T(8,128)}) fusion(pred[512]{0:T(512)(128)(4,1)S(1)} %broadcast_in_dim.133, bf16[128,4,16,128]{0,3,2,1:T(8,128)(2,1)} %bitcast.111, bf16[512,1,4,128]{3,2,1,0:T(4,128)(2,1)S(1)} %get-tuple-element.59), kind=kOutput, calls=%fused_computation.4 | convolution fusion | flops 1086316544 | bytes 19431936 | tf_op jit(solution)/shard_map/while/body/eval_jaxpr/qkgd,rkd->qkgr/dot_general | solution.py:89
  66.9 0.0 copy-done
  66.9 2.9 %fusion.15 = (f32[128,4,16]{0,2,1:T(8,128)S(1)}, f32[4,136,128,16]{2,1,3,0:T(8,128)}) fusion(pred[128,136]{0,1:T(8,128)(4,1)S(1)} %pad_add_fusion, bf16[128,4,16,128]{0,3,2,1:T(8,128)(2,1)S(1)} %bitcast.112, bf16[128,2,4,128]{3,0,2,1:T(8,128)(2,1)S(1)} %copy_select_fusion, bf16[8,2,4,128]{3,0,2,1:T(8,128)(2,1)S(1)} %copy.131), kind=kOutput, calls=%fused_computation.25 | convolution fusion | flops 288825344 | bytes 6882304 | tf_op jit(solution)/shard_map/while/body/eval_jaxpr/qkgd,rkd->qkgr/dot_general | solution.py:89
  69.8 0.8 broadcast_in_dim.138
  70.7 0.0 slice-start
  70.7 5.1 %all-to-all-start.1 = ((f32[16,128,4,16]{1,3,2,0:T(8,128)}), f32[16,128,4,16]{1,3,2,0:T(8,128)S(1)}, u32[]{:S(2)}, u32[]{:S(2)}) async-start(f32[16,128,4,16]{1,3,2,0:T(8,128)} %broadcast_in_dim.138), calls=%async_computation.1 | async-start | bytes 1048576 | tf_op jit(solution)/shard_map/all_to_all | solution.py:26
  75.8 0.0 slice-start.1
  75.8 8.5 %fusion.2 = f32[128,4,16]{0,2,1:T(8,128)S(1)} fusion(f32[4,512,128,16]{2,1,3,0:T(8,128)} %get-tuple-element.69, f32[128,4,16]{0,2,1:T(8,128)S(1)} %get-tuple-element.62, pred[512]{0:T(512)(128)(4,1)S(1)} %broadcast_in_dim.133), kind=kLoop, calls=%fused_computation.8 | loop fusion | flops 20963328 | bytes 16843264 | tf_op jit(solution)/shard_map/while/body/eval_jaxpr/reduce_sum | solution.py:99
  84.3 0.0 slice-done
  84.3 0.0 slice-done.1
  84.3 1.3 fusion.16
  85.6 0.0 copy-start.2
  85.7 5.3 %fusion.17 = f32[4,128,128,16]{2,1,3,0:T(8,128)} fusion(f32[4,136,128,16]{2,1,3,0:T(8,128)S(1)} %bitcast.110, f32[128,4,16]{0,2,1:T(8,128)S(1)} %get-tuple-element.65, pred[128,136]{0,1:T(8,128)(4,1)S(1)} %pad_add_fusion, bf16[8,2,4,128]{3,0,2,1:T(8,128)(2,1)S(1)} %copy.131, bf16[128,2,4,128]{3,0,2,1:T(8,128)(2,1)S(1)} %copy_select_fusion), kind=kOutput, calls=%fused_computation.27 | convolution fusion | flops 1716011008 | bytes 8979456 | tf_op jit(solution)/shard_map/while/body/eval_jaxpr/qkgr,rkd->qkgd/dot_general | solution.py:101
  90.9 0.0 all-to-all-done.1
  91.0 0.0 copy-done.2
  91.0 15.8 %fusion.13 = f32[128,4,16,128]{0,3,2,1:T(8,128)S(1)} fusion(f32[4,128,128,16]{2,1,3,0:T(8,128)} %fusion.17, f32[4,512,128,16]{2,1,3,0:T(8,128)} %get-tuple-element.69, f32[128,4,16]{0,2,1:T(8,128)S(1)} %get-tuple-element.62, pred[512]{0:T(512)(128)(4,1)S(1)} %broadcast_in_dim.133, f32[128,4,16]{0,2,1:T(8,128)S(1)} %get-tuple-element.64, ...), kind=kOutput, calls=%fused_computation.22 | convolution fusion | flops 6465519616 | bytes 25887232 | tf_op jit(solution)/shard_map/while/body/eval_jaxpr/qkgr,rkd->qkgd/dot_general | solution.py:101
  106.8 2.8 %copy.141 = f32[128,16,4,128]{0,2,3,1:T(4,128)S(1)} copy(f32[128,16,4,128]{0,3,2,1:T(8,128)S(1)} %bitcast.113) | data formatting | bytes 8388608 | tf_op jit(solution)/shard_map/concatenate | solution.py:49
  109.6 0.1 exponential_multiply_fusion
  109.6 3.0 %maximum_bitcast_fusion = f32[16,128,4,129]{1,2,3,0:T(4,128)} fusion(f32[128,16,4,1]{0,2,3,1:T(4,128)S(1)} %exponential_multiply_fusion, f32[128,16,4,128]{0,2,3,1:T(4,128)S(1)} %copy.141), kind=kLoop, calls=%fused_computation.18 | loop fusion | flops 1056768 | bytes 8454144 | tf_op jit(solution)/shard_map/transpose | solution.py:38
  112.6 7.3 %all-to-all-start.2 = ((f32[16,128,4,129]{1,2,3,0:T(4,128)}), f32[16,128,4,129]{1,2,3,0:T(4,128)}, u32[]{:S(2)}, u32[]{:S(2)}) async-start(f32[16,128,4,129]{1,2,3,0:T(4,128)} %maximum_bitcast_fusion), calls=%async_computation.2 | async-start | bytes 8454144 | tf_op jit(solution)/shard_map/all_to_all | solution.py:43
  120.5 0.0 copy-start.1
  120.5 59.2 %all-to-all-done.2 = f32[16,128,4,129]{1,2,3,0:T(4,128)} async-done(((f32[16,128,4,129]{1,2,3,0:T(4,128)}), f32[16,128,4,129]{1,2,3,0:T(4,128)}, u32[]{:S(2)}, u32[]{:S(2)}) %all-to-all-start.2) | async-done | bytes 4227104 | tf_op jit(solution)/shard_map/all_to_all | solution.py:43
  179.7 2.9 %reduce_sum.63 = f32[128,4,129]{0,1,2:T(4,128)S(1)} reduce(f32[16,128,4,129]{1,2,3,0:T(4,128)} %all-to-all-done.2, f32[]{:T(128)} %constant.52.clone.1), dimensions={0}, to_apply=%region_7.8 | reduce | flops 990720 | bytes 4491268 | tf_op jit(solution)/shard_map/reduce_sum | solution.py:44
  182.6 0.8 copy.143
  183.4 0.0 copy-done.1
  (19 shorter events, 0.2 us)
Async XLA Ops:
  7.2 50.9 %all-gather.3.cloned.1.call-start = ((), (), s32[]{:S(2)}) async-start(), calls=%async_computation.3 | async-start | bytes 2228224 | tf_op jit(solution)/shard_map/all_gather | solution.py:122
  14.6 9.0 %copy-start.4 = (s32[1,4]{1,0:T(1,128)S(1)}, s32[1,4]{1,0:T(1,128)}, u32[]{:S(2)}) copy-start(s32[1,4]{1,0:T(1,128)} %param.11) | copy-start | bytes 52
  14.6 9.8 %copy-start.3 = (bf16[1,8,2,512]{3,2,1,0:T(2,128)(2,1)S(1)}, bf16[1,8,2,512]{3,2,1,0:T(2,128)(2,1)}, u32[]{:S(2)}) copy-start(bf16[1,8,2,512]{3,2,1,0:T(2,128)(2,1)} %param.9) | copy-start | bytes 49156
  18.2 21.4 %all-to-all-start = ((bf16[8,2,32769]{2,1,0:T(2,128)(2,1)}), bf16[8,2,32769]{2,1,0:T(2,128)(2,1)S(1)}, u32[]{:S(2)}, u32[]{:S(2)}) async-start(bf16[8,2,32769]{2,1,0:T(2,128)(2,1)} %pad_maximum_fusion), calls=%async_computation | async-start | bytes 2105344 | tf_op jit(solution)/shard_map/all_to_all | solution.py:17
  58.0 8.9 %copy-start = (bf16[1,128,8192]{1,2,0:T(8,128)(2,1)S(1)}, bf16[1,128,8192]{1,2,0:T(8,128)(2,1)}, u32[]{:S(2)}) copy-start(bf16[1,128,8192]{1,2,0:T(8,128)(2,1)} %all-gather.3.cloned.1.call-done) | copy-start | bytes 6291460
  70.7 13.6 %slice-start = ((s8[4456448]{0:T(1024)(128)(4,1)}), s8[262144]{0:T(1024)(128)(4,1)S(1)}, s32[]{:S(2)}) async-start(s8[4456448]{0:T(1024)(128)(4,1)} %bitcast.109), calls=%async_computation.4 | async-start | bytes 524288
  70.7 20.2 %all-to-all-start.1 = ((f32[16,128,4,16]{1,3,2,0:T(8,128)}), f32[16,128,4,16]{1,3,2,0:T(8,128)S(1)}, u32[]{:S(2)}, u32[]{:S(2)}) async-start(f32[16,128,4,16]{1,3,2,0:T(8,128)} %broadcast_in_dim.138), calls=%async_computation.1 | async-start | bytes 1048576 | tf_op jit(solution)/shard_map/all_to_all | solution.py:26
  75.8 8.6 %slice-start.1 = ((s8[4456448]{0:T(1024)(128)(4,1)}), s8[4194304]{0:T(1024)(128)(4,1)S(1)}, s32[]{:S(2)}) async-start(s8[4456448]{0:T(1024)(128)(4,1)} %bitcast.109), calls=%async_computation.5 | async-start | bytes 8388608
  85.6 5.3 %copy-start.2 = (bf16[512,1,4,128]{0,3,2,1:T(8,128)(2,1)S(1)}, bf16[512,1,4,128]{0,3,2,1:T(8,128)(2,1)}, u32[]{:S(2)}) copy-start(bf16[512,1,4,128]{0,3,2,1:T(8,128)(2,1)} %copy.158) | copy-start | bytes 1572868
  112.6 67.1 %all-to-all-start.2 = ((f32[16,128,4,129]{1,2,3,0:T(4,128)}), f32[16,128,4,129]{1,2,3,0:T(4,128)}, u32[]{:S(2)}, u32[]{:S(2)}) async-start(f32[16,128,4,129]{1,2,3,0:T(4,128)} %maximum_bitcast_fusion), calls=%async_computation.2 | async-start | bytes 8454144 | tf_op jit(solution)/shard_map/all_to_all | solution.py:43
  120.5 62.9 %copy-start.1 = (bf16[1,12,32,2,512]{4,3,2,1,0:T(2,128)(2,1)}, bf16[1,12,32,2,512]{4,3,2,1,0:T(2,128)(2,1)S(1)}, u32[]{:S(2)}) copy-start(bf16[1,12,32,2,512]{4,3,2,1,0:T(2,128)(2,1)S(1)} %bitcast_dynamic-update-slice_fusion) | copy-start | bytes 2359300
Sparse Core Ops, SparseCore 0:
  10.7 47.2 all-gather.2
where the time goes:
time: 191 us; the launch traced here: 190 us
  waiting for transfers between devices  87.8 us (46%)
  matrix products  33.4 us (17%)
  other arithmetic  21 us (11%)
  starting transfers between devices  17.8 us (9%)
  between operations  15.6 us (8%)
  local copies, waits for them, and re-layouts  14.7 us (8%)
    all_to_all x1, waiting for transfers between devices, sum_at_owner(): lax.all_to_all(split_up(value, dim, length), axis, 0, 0, tiled=True)  59.2 us
    dot_general x2, matrix products, block_step(): jnp.einsum('qkgr,rkd->qkgd', weights, block_values, precision=lax.Precisi...  21 us
    all_gather x1, waiting for transfers between devices, local(): gathered = lax.all_gather(queries[0], 'aa', axis=1, tiled=True)  15 us
    all_to_all x1, waiting for transfers between devices, in_one_piece(): lax.all_to_all(both, axis, split_axis=split_dim, concat_axis=concat_dim,...  13.6 us
    dot_general x2, matrix products, block_step(): jnp.einsum('qkgd,rkd->qkgr', query_heads, block_keys[:, 0], preferred_ele...  11.8 us
    reduce_sum x2, other arithmetic, block_step(): new_sum = run_sum * shrink + jnp.sum(weights, axis=-1)  9.83 us
    all_to_all x1, starting transfers between devices, sum_at_owner(): lax.all_to_all(split_up(value, dim, length), axis, 0, 0, tiled=True)  7.25 us
    all_to_all x1, starting transfers between devices, in_one_piece(): lax.all_to_all(both, axis, split_axis=split_dim, concat_axis=concat_dim,...  5.39 us
  transfers between devices with their start and end apart: 4, of which 3 were waited for; matrix products, arithmetic and copies ran while one was open for 15% of the time, Pallas kernels for 0%

commit v1 on v0

--- a/solution.py
+++ b/solution.py
@@ -119,7 +119,9 @@
     page_rows = pool_pages.shape[1]
     kv_width = pool_pages.shape[-1]
     kv_heads = kv_width // HEAD_DIM
-    gathered = lax.all_gather(queries[0], "aa", axis=1, tiled=True)
+    gathered = jnp.concatenate(
+        lax.all_to_all(jnp.stack([queries[0]] * lax.axis_size("aa")), "aa", 0, 0), axis=1
+    )
     query_count = gathered.shape[0]
     query_heads = gathered.reshape(query_count, kv_heads, -1, HEAD_DIM)
     moved_ids = move_page[0]

time: 191 us -> 197 us (1.031)
  between operations: 15.6 us -> 2.23 us
  waiting for transfers between devices: 87.8 us -> 95 us
  local copies, waits for them, and re-layouts: 14.7 us -> 20.6 us
  starting transfers between devices: 17.8 us -> 23.5 us
    all_to_all x0 -> x1, waiting for transfers between devices: none -> 19.2 us  [local(): lax.all_to_all(jnp.stack([queries[0]] * lax.axis_size('aa')), 'aa', 0, 0)]
    all_gather x1 -> x0, waiting for transfers between devices: 15 us -> none  [local(): gathered = lax.all_gather(queries[0], 'aa', axis=1, tiled=True)]
    all_to_all x0 -> x1, starting transfers between devices: none -> 7.03 us  [local(): lax.all_to_all(jnp.stack([queries[0]] * lax.axis_size('aa')), 'aa', 0, 0)]
    all_to_all x1, waiting for transfers between devices: 13.6 us -> 15.9 us  [in_one_piece(): lax.all_to_all(both, axis, split_axis=split_dim, concat_axis=concat_dim,...]
    unnamed x19 -> x16, local copies, waits for them, and re-layouts: 4.82 us -> 3.34 us
  transfers between devices with their start and end apart: 4 -> 4, of which waited for: 3 -> 3; matrix products, arithmetic and copies ran while one was open for 15% -> 14% of each run, Pallas kernels for 0% -> 0%
where the time goes in v1:
time: 197 us; the launch traced here: 196 us
  waiting for transfers between devices  95 us (48%)
  matrix products  32.6 us (17%)
  starting transfers between devices  23.5 us (12%)
  other arithmetic  22 us (11%)
  local copies, waits for them, and re-layouts  20.6 us (10%)
  between operations  2.23 us (1%)
    all_to_all x1, waiting for transfers between devices, sum_at_owner(): lax.all_to_all(split_up(value, dim, length), axis, 0, 0, tiled=True)  59.9 us
    dot_general x2, matrix products, block_step(): jnp.einsum('qkgr,rkd->qkgd', weights, block_values, precision=lax.Precisi...  21 us
    all_to_all x1, waiting for transfers between devices, local(): lax.all_to_all(jnp.stack([queries[0]] * lax.axis_size('aa')), 'aa', 0, 0)  19.2 us
    all_to_all x1, waiting for transfers between devices, in_one_piece(): lax.all_to_all(both, axis, split_axis=split_dim, concat_axis=concat_dim,...  15.9 us
    dot_general x2, matrix products, block_step(): jnp.einsum('qkgd,rkd->qkgr', query_heads, block_keys[:, 0], preferred_ele...  11 us
    reduce_sum x2, other arithmetic, block_step(): new_sum = run_sum * shrink + jnp.sum(weights, axis=-1)  9.83 us
    all_to_all x1, starting transfers between devices, local(): lax.all_to_all(jnp.stack([queries[0]] * lax.axis_size('aa')), 'aa', 0, 0)  7.03 us
    all_to_all x1, starting transfers between devices, sum_at_owner(): lax.all_to_all(split_up(value, dim, length), axis, 0, 0, tiled=True)  7.01 us
  transfers between devices with their start and end apart: 4, of which 3 were waited for; matrix products, arithmetic and copies ran while one was open for 14% of the time, Pallas kernels for 0%

profile of v1, /device:TPU:0, one launch (start us, length us, event | category | flops | bytes accessed | tf_op | source)
XLA Modules:
  0.0 195.8 jit_solution(16042661867917780158)
XLA Ops:
  0.6 1.1 copy.173
  1.8 0.0 copy-start
  1.8 0.7 fusion.45
  2.4 0.7 compare_and_fusion
  3.1 0.9 convert_reduce_fusion
  4.0 0.7 fusion.46
  4.7 0.1 fusion.42
  4.8 0.1 reshape_reshape.13
  4.8 1.5 gather_fusion.1
  6.3 0.0 copy-done
  6.3 0.0 copy-start.1
  6.4 0.3 gather.15
  6.7 0.6 convolution_convert_fusion
  7.3 0.7 reshape_reshape.11
  8.0 1.9 pad_maximum_fusion
  9.9 0.0 copy-start.3
  9.9 0.0 copy-start.2
  9.9 5.5 %all-to-all-start.1 = ((bf16[8,2,32769]{2,1,0:T(2,128)(2,1)}), bf16[8,2,32769]{2,1,0:T(2,128)(2,1)S(1)}, u32[]{:S(2)}, u32[]{:S(2)}) async-start(bf16[8,2,32769]{2,1,0:T(2,128)(2,1)} %pad_maximum_fusion), calls=%async_computation.1 | async-start | bytes 2105344 | tf_op jit(solution)/shard_map/all_to_all | solution.py:17
  15.5 0.0 copy-done.1
  15.5 0.1 copy.132
  15.6 15.9 %all-to-all-done.1 = bf16[8,2,32769]{2,1,0:T(2,128)(2,1)S(1)} async-done(((bf16[8,2,32769]{2,1,0:T(2,128)(2,1)}), bf16[8,2,32769]{2,1,0:T(2,128)(2,1)S(1)}, u32[]{:S(2)}, u32[]{:S(2)}) %all-to-all-start.1) | async-done | bytes 1048640 | tf_op jit(solution)/shard_map/all_to_all | solution.py:17
  31.5 1.8 stack.3
  33.2 7.0 %all-to-all-start = ((bf16[16,128,512]{1,2,0:T(8,128)(2,1)}), bf16[16,128,512]{1,2,0:T(8,128)(2,1)S(1)}, u32[]{:S(2)}, u32[]{:S(2)}) async-start(bf16[16,128,512]{1,2,0:T(8,128)(2,1)} %stack.3), calls=%async_computation | async-start | bytes 4194304 | tf_op jit(solution)/shard_map/all_to_all | solution.py:123
  40.9 0.0 copy-done.3
  40.9 0.1 broadcast_in_dim.123
  41.0 0.1 broadcast_in_dim.124
  41.1 0.0 copy-done.2
  41.2 2.2 %gather_fusion = bf16[4,32,2,512]{3,2,1,0:T(2,128)(2,1)S(1)} fusion(bf16[12,32,2,512]{3,2,1,0:T(2,128)(2,1)} %bitcast.118, s32[1024]{0:T(1024)S(1)} %pad_clamp_fusion.1), kind=kCustom, calls=%fused_computation | custom fusion | bytes 524304 | tf_op jit(solution)/shard_map/jit(_take)/gather | solution.py:147
  43.4 0.9 reshape.296
  44.3 0.1 iota_compare_fusion.3
  44.4 0.1 pad_add_fusion
  44.5 1.0 copy_select_fusion
  45.5 0.1 copy.156
  45.6 1.8 split.17
  47.4 1.8 squeeze.59
  49.3 1.3 fusion.58
  50.6 1.3 copy.158
  51.9 0.1 copy.136
  52.0 0.1 broadcast_in_dim.132
  52.1 0.1 broadcast_in_dim.133
  52.2 19.2 %all-to-all-done = bf16[16,128,512]{1,2,0:T(8,128)(2,1)S(1)} async-done(((bf16[16,128,512]{1,2,0:T(8,128)(2,1)}), bf16[16,128,512]{1,2,0:T(8,128)(2,1)S(1)}, u32[]{:S(2)}, u32[]{:S(2)}) %all-to-all-start) | async-done | bytes 2097184 | tf_op jit(solution)/shard_map/all_to_all | solution.py:123
  71.4 8.1 %bitcast_reduce_fusion = (f32[128,4,16]{0,2,1:T(8,128)S(1)}, f32[4,512,128,16]{2,1,3,0:T(8,128)}) fusion(pred[512]{0:T(512)(128)(4,1)S(1)} %broadcast_in_dim.133, bf16[128,4,16,128]{0,3,2,1:T(8,128)(2,1)S(1)} %bitcast.114, bf16[512,1,4,128]{3,2,1,0:T(4,128)(2,1)} %get-tuple-element.59), kind=kOutput, calls=%fused_computation.4 | convolution fusion | flops 1086316544 | bytes 19431936 | tf_op jit(solution)/shard_map/while/body/eval_jaxpr/qkgd,rkd->qkgr/dot_general | solution.py:89
  79.5 2.9 %fusion.15 = (f32[128,4,16]{0,2,1:T(8,128)S(1)}, f32[4,136,128,16]{2,1,3,0:T(8,128)}) fusion(pred[128,136]{0,1:T(8,128)(4,1)S(1)} %pad_add_fusion, bf16[128,4,16,128]{0,3,2,1:T(8,128)(2,1)S(1)} %bitcast.115, bf16[128,2,4,128]{3,0,2,1:T(8,128)(2,1)S(1)} %copy_select_fusion, bf16[8,2,4,128]{3,0,2,1:T(8,128)(2,1)S(1)} %copy.131), kind=kOutput, calls=%fused_computation.25 | convolution fusion | flops 288825344 | bytes 6882304 | tf_op jit(solution)/shard_map/while/body/eval_jaxpr/qkgd,rkd->qkgr/dot_general | solution.py:89
  82.4 0.8 broadcast_in_dim.138
  83.2 0.0 slice-start
  83.2 3.9 %all-to-all-start.2 = ((f32[16,128,4,16]{1,3,2,0:T(8,128)}), f32[16,128,4,16]{1,3,2,0:T(8,128)S(1)}, u32[]{:S(2)}, u32[]{:S(2)}) async-start(f32[16,128,4,16]{1,3,2,0:T(8,128)} %broadcast_in_dim.138), calls=%async_computation.2 | async-start | bytes 1048576 | tf_op jit(solution)/shard_map/all_to_all | solution.py:26
  87.1 0.0 slice-start.1
  87.1 8.5 %fusion.2 = f32[128,4,16]{0,2,1:T(8,128)S(1)} fusion(f32[4,512,128,16]{2,1,3,0:T(8,128)} %get-tuple-element.69, f32[128,4,16]{0,2,1:T(8,128)S(1)} %get-tuple-element.62, pred[512]{0:T(512)(128)(4,1)S(1)} %broadcast_in_dim.133), kind=kLoop, calls=%fused_computation.8 | loop fusion | flops 20963328 | bytes 16843264 | tf_op jit(solution)/shard_map/while/body/eval_jaxpr/reduce_sum | solution.py:99
  95.7 0.0 slice-done
  95.7 0.0 slice-done.1
  95.7 1.3 fusion.16
  97.0 5.3 %fusion.17 = f32[4,128,128,16]{2,1,3,0:T(8,128)} fusion(f32[4,136,128,16]{2,1,3,0:T(8,128)S(1)} %bitcast.113, f32[128,4,16]{0,2,1:T(8,128)S(1)} %get-tuple-element.65, pred[128,136]{0,1:T(8,128)(4,1)S(1)} %pad_add_fusion, bf16[8,2,4,128]{3,0,2,1:T(8,128)(2,1)S(1)} %copy.131, bf16[128,2,4,128]{3,0,2,1:T(8,128)(2,1)S(1)} %copy_select_fusion), kind=kOutput, calls=%fused_computation.27 | convolution fusion | flops 1716011008 | bytes 8979456 | tf_op jit(solution)/shard_map/while/body/eval_jaxpr/qkgr,rkd->qkgd/dot_general | solution.py:101
  102.3 0.0 all-to-all-done.2
  102.3 15.8 %fusion.13 = f32[128,4,16,128]{0,3,2,1:T(8,128)S(1)} fusion(f32[4,128,128,16]{2,1,3,0:T(8,128)} %fusion.17, f32[4,512,128,16]{2,1,3,0:T(8,128)} %get-tuple-element.69, f32[128,4,16]{0,2,1:T(8,128)S(1)} %get-tuple-element.62, pred[512]{0:T(512)(128)(4,1)S(1)} %broadcast_in_dim.133, f32[128,4,16]{0,2,1:T(8,128)S(1)} %get-tuple-element.64, ...), kind=kOutput, calls=%fused_computation.22 | convolution fusion | flops 6465519616 | bytes 25887232 | tf_op jit(solution)/shard_map/while/body/eval_jaxpr/qkgr,rkd->qkgd/dot_general | solution.py:101
  118.1 2.8 %copy.141 = f32[128,16,4,128]{0,2,3,1:T(4,128)S(1)} copy(f32[128,16,4,128]{0,3,2,1:T(8,128)S(1)} %bitcast.116) | data formatting | bytes 8388608 | tf_op jit(solution)/shard_map/concatenate | solution.py:49
  120.9 0.1 exponential_multiply_fusion
  121.0 3.0 %maximum_bitcast_fusion = f32[16,128,4,129]{1,2,3,0:T(4,128)} fusion(f32[128,16,4,1]{0,2,3,1:T(4,128)S(1)} %exponential_multiply_fusion, f32[128,16,4,128]{0,2,3,1:T(4,128)S(1)} %copy.141), kind=kLoop, calls=%fused_computation.18 | loop fusion | flops 1056768 | bytes 8454144 | tf_op jit(solution)/shard_map/transpose | solution.py:38
  123.9 7.0 %all-to-all-start.3 = ((f32[16,128,4,129]{1,2,3,0:T(4,128)}), f32[16,128,4,129]{1,2,3,0:T(4,128)}, u32[]{:S(2)}, u32[]{:S(2)}) async-start(f32[16,128,4,129]{1,2,3,0:T(4,128)} %maximum_bitcast_fusion), calls=%async_computation.3 | async-start | bytes 8454144 | tf_op jit(solution)/shard_map/all_to_all | solution.py:43
  131.6 0.6 bitcast_dynamic-update-slice_fusion
  132.2 59.9 %all-to-all-done.3 = f32[16,128,4,129]{1,2,3,0:T(4,128)} async-done(((f32[16,128,4,129]{1,2,3,0:T(4,128)}), f32[16,128,4,129]{1,2,3,0:T(4,128)}, u32[]{:S(2)}, u32[]{:S(2)}) %all-to-all-start.3) | async-done | bytes 4227104 | tf_op jit(solution)/shard_map/all_to_all | solution.py:43
  192.1 2.9 %reduce_sum.63 = f32[128,4,129]{0,1,2:T(4,128)S(1)} reduce(f32[16,128,4,129]{1,2,3,0:T(4,128)} %all-to-all-done.3, f32[]{:T(128)} %constant.52.clone.1), dimensions={0}, to_apply=%region_7.8 | reduce | flops 990720 | bytes 4491268 | tf_op jit(solution)/shard_map/reduce_sum | solution.py:44
  195.1 0.8 copy.143
  (18 shorter events, 0.2 us)
Async XLA Ops:
  1.8 4.6 %copy-start = (bf16[1,12,32,2,512]{4,3,2,1,0:T(2,128)(2,1)}, bf16[1,12,32,2,512]{4,3,2,1,0:T(2,128)(2,1)S(1)}, u32[]{:S(2)}) copy-start(bf16[1,12,32,2,512]{4,3,2,1,0:T(2,128)(2,1)S(1)} %copy.173) | copy-start | bytes 2359300
  6.3 9.1 %copy-start.1 = (bf16[1,128,512]{2,1,0:T(8,128)(2,1)S(1)}, bf16[1,128,512]{2,1,0:T(8,128)(2,1)}, u32[]{:S(2)}) copy-start(bf16[1,128,512]{2,1,0:T(8,128)(2,1)} %param.8) | copy-start | bytes 393220
  9.9 31.0 %copy-start.3 = (s32[1,4]{1,0:T(1,128)S(1)}, s32[1,4]{1,0:T(1,128)}, u32[]{:S(2)}) copy-start(s32[1,4]{1,0:T(1,128)} %param.11) | copy-start | bytes 52
  9.9 31.2 %copy-start.2 = (bf16[1,8,2,512]{3,2,1,0:T(2,128)(2,1)S(1)}, bf16[1,8,2,512]{3,2,1,0:T(2,128)(2,1)}, u32[]{:S(2)}) copy-start(bf16[1,8,2,512]{3,2,1,0:T(2,128)(2,1)} %param.9) | copy-start | bytes 49156
  9.9 21.5 %all-to-all-start.1 = ((bf16[8,2,32769]{2,1,0:T(2,128)(2,1)}), bf16[8,2,32769]{2,1,0:T(2,128)(2,1)S(1)}, u32[]{:S(2)}, u32[]{:S(2)}) async-start(bf16[8,2,32769]{2,1,0:T(2,128)(2,1)} %pad_maximum_fusion), calls=%async_computation.1 | async-start | bytes 2105344 | tf_op jit(solution)/shard_map/all_to_all | solution.py:17
  33.2 38.2 %all-to-all-start = ((bf16[16,128,512]{1,2,0:T(8,128)(2,1)}), bf16[16,128,512]{1,2,0:T(8,128)(2,1)S(1)}, u32[]{:S(2)}, u32[]{:S(2)}) async-start(bf16[16,128,512]{1,2,0:T(8,128)(2,1)} %stack.3), calls=%async_computation | async-start | bytes 4194304 | tf_op jit(solution)/shard_map/all_to_all | solution.py:123
  83.2 12.5 %slice-start = ((s8[4456448]{0:T(1024)(128)(4,1)}), s8[262144]{0:T(1024)(128)(4,1)S(1)}, s32[]{:S(2)}) async-start(s8[4456448]{0:T(1024)(128)(4,1)} %bitcast.112), calls=%async_computation.4 | async-start | bytes 524288
  83.2 19.0 %all-to-all-start.2 = ((f32[16,128,4,16]{1,3,2,0:T(8,128)}), f32[16,128,4,16]{1,3,2,0:T(8,128)S(1)}, u32[]{:S(2)}, u32[]{:S(2)}) async-start(f32[16,128,4,16]{1,3,2,0:T(8,128)} %broadcast_in_dim.138), calls=%async_computation.2 | async-start | bytes 1048576 | tf_op jit(solution)/shard_map/all_to_all | solution.py:26
  87.1 8.6 %slice-start.1 = ((s8[4456448]{0:T(1024)(128)(4,1)}), s8[4194304]{0:T(1024)(128)(4,1)S(1)}, s32[]{:S(2)}) async-start(s8[4456448]{0:T(1024)(128)(4,1)} %bitcast.112), calls=%async_computation.5 | async-start | bytes 8388608
  123.9 68.2 %all-to-all-start.3 = ((f32[16,128,4,129]{1,2,3,0:T(4,128)}), f32[16,128,4,129]{1,2,3,0:T(4,128)}, u32[]{:S(2)}, u32[]{:S(2)}) async-start(f32[16,128,4,129]{1,2,3,0:T(4,128)} %maximum_bitcast_fusion), calls=%async_computation.3 | async-start | bytes 8454144 | tf_op jit(solution)/shard_map/all_to_all | solution.py:43
